TPU v7x, 32 devices: a whole 2x2x4 slice. The times are simulated.
32 devices in a mesh: row: 4 (over z), col: 4 (over y, core), ch: 2 (over x).
Axes of the slice: x: 2, y: 2, z: 4, core: 2. Of those that a mesh axis runs over, the one named last changes fastest.
Arguments:
- spectra: float32 [384, 128, 1024], P('ch', 'row', 'col'), may hold values from 0 to 1
- pixel_factor: float32 [64, 128, 1024], P(None, 'row', 'col'), may hold values from 0.1 to 1
- channel_factor: float32 [64, 384], P(None, 'ch'), may hold values from 0.1 to 1
- labels: int32 [128, 1024], P('row', 'col'), may hold values from 0 to 3
Outputs:
- smoothed_factor: float32 [64, 128, 1024], P(None, 'row', 'col')
- new_channel: float32 [64, 384], P(None, 'ch')
All inputs are finite; a program needn't handle non-finite values.
Results may differ from a plain program's by a relative error of at most 0.000068.
Values sent between devices are 32-bit elements; how exact they have to be, the bound alone decides.
A program may use at most 64 MiB of HBM per device.

v0:
```python
import jax
import jax.numpy as jnp
from jax import lax
from jax.sharding import PartitionSpec as P

SMOOTH = 3
epsilon = 1e-09


def padded_2(block, sides, width):
    for axis, dim in sides:
        count = lax.axis_size(axis)
        forward = [(i, i + 1) for i in range(count - 1)]
        backward = [(target, source) for source, target in forward]
        low = lax.ppermute(
            lax.slice_in_dim(block, block.shape[dim] - width, None, axis=dim), axis, forward
        )
        high = lax.ppermute(lax.slice_in_dim(block, 0, width, axis=dim), axis, backward)
        block = jnp.concatenate([low, block, high], axis=dim)
    return block


def coefficients(marked):
    center = marked[1:-1, 1:-1]
    result = []
    for neighbour in (marked[:-2, 1:-1], marked[2:, 1:-1], marked[1:-1, :-2], marked[1:-1, 2:]):
        result.append(
            jnp.where(neighbour == 0, 0.0, jnp.where(neighbour == center, 1.0, 0.25)).astype(
                jnp.float32
            )
        )
    return result


def smooth_once(padded, field, weights):
    combined = field + weights[0] * padded[:, :-2, 1:-1] + weights[1] * padded[:, 2:, 1:-1]
    combined = combined + weights[2] * padded[:, 1:-1, :-2] + weights[3] * padded[:, 1:-1, 2:]
    return combined / (1.0 + weights[0] + weights[1] + weights[2] + weights[3])


def lift_factor(own_factor, pixel_top, chan_gram):
    factor_rank = own_factor.shape[0]
    flat_own = own_factor.reshape(factor_rank, -1)
    lower = jnp.dot(
        chan_gram, flat_own, precision=lax.Precision.HIGHEST, preferred_element_type=jnp.float32
    )
    return (flat_own * pixel_top.reshape(factor_rank, -1) / (lower + epsilon)).reshape(
        own_factor.shape
    )


def shards(spectra, pixel_factor, channel_factor, labels):
    precise = lax.Precision.HIGHEST
    contraction = (((1,), (1,)), ((), ()))
    factor_rank, row_count, col_count = pixel_factor.shape
    flat_pixel = pixel_factor.reshape(factor_rank, row_count * col_count)
    flat_data = spectra.reshape(spectra.shape[0], row_count * col_count)
    chan_top = lax.dot_general(
        flat_pixel, flat_data, contraction, precision=precise, preferred_element_type=jnp.float32
    )
    pixel_gram = lax.dot_general(
        flat_pixel, flat_pixel, contraction, precision=precise, preferred_element_type=jnp.float32
    )
    chan_top, pixel_gram = lax.psum((chan_top, pixel_gram), ("row", "col"))
    new_channel = (
        channel_factor
        * chan_top
        / (
            jnp.dot(
                pixel_gram, channel_factor, precision=precise, preferred_element_type=jnp.float32
            )
            + epsilon
        )
    )
    part_top = jnp.dot(
        new_channel, flat_data, precision=precise, preferred_element_type=jnp.float32
    ).reshape(factor_rank, row_count, col_count)
    part_gram = lax.dot_general(
        new_channel, new_channel, contraction, precision=precise, preferred_element_type=jnp.float32
    )
    marked = labels + 1
    share_rows = row_count // lax.axis_size("ch")
    share_start = lax.axis_index("ch") * share_rows
    pixel_top = lax.psum_scatter(part_top, "ch", scatter_dimension=1, tiled=True)
    chan_gram = lax.psum(part_gram, "ch")
    own_factor = lax.dynamic_slice_in_dim(pixel_factor, share_start, share_rows, 1)
    own_marks = lax.dynamic_slice_in_dim(marked, share_start, share_rows, 0)
    field = lift_factor(own_factor, pixel_top, chan_gram)
    border_marks = padded_2(own_marks, ((("row", "ch"), 0), ("col", 1)), 1)
    weights = coefficients(border_marks)
    for iteration in range(SMOOTH):
        padded = padded_2(field, ((("row", "ch"), 1), ("col", 2)), 1)
        field = smooth_once(padded, field, weights)
    smoothed_factor = lax.all_gather(field, "ch", axis=1, tiled=True)
    return (smoothed_factor, new_channel)


def solution(mesh):
    placed = (P("ch", "row", "col"), P(None, "row", "col"), P(None, "ch"), P("row", "col"))
    return jax.shard_map(
        shards,
        mesh=mesh,
        in_specs=placed,
        out_specs=(P(None, "row", "col"), P(None, "ch")),
        check_vma=False,
    )
```

profile of v0, /device:TPU:0, one launch (start us, length us, event | category | flops | bytes accessed | tf_op | source)
XLA Modules:
  0.0 290.6 jit_solution(9528814193666715446)
XLA Ops:
  7.2 7.0 %fusion.42 = f32[64,64]{1,0:T(8,128)} fusion(f32[64,32,256]{2,1,0:T(8,128)} %param.5), kind=kOutput, calls=%fused_computation.64 | convolution fusion | flops 402653184 | bytes 2113536 | tf_op jit(solution)/shard_map/dot_general | solution.py:61
  14.2 12.2 %fusion.36 = f32[64,192]{1,0:T(8,128)} fusion(f32[192,32,256]{2,1,0:T(8,128)} %param.4, f32[64,32,256]{2,1,0:T(8,128)S(1)} %copy-done.2), kind=kOutput, calls=%fused_computation.61 | convolution fusion | flops 1207959552 | bytes 8437760 | tf_op jit(solution)/shard_map/dot_general | solution.py:58
  26.5 0.2 reduce-scatter.2.cloned.1.call-start
  26.7 91.5 %all-reduce.3.cloned.1.call-done = (f32[64,64]{1,0:T(8,128)}, f32[64,192]{1,0:T(8,128)}) async-done(((f32[64,64]{1,0:T(8,128)}, f32[64,192]{1,0:T(8,128)}), (f32[64,64]{1,0:T(8,128)}, f32[64,192]{1,0:T(8,128)})) %all-reduce.3.cloned.1.call-update) | async-done | bytes 65552 | tf_op jit(solution)/shard_map/psum | solution.py:64
  118.2 1.1 fusion.41
  119.3 11.4 %fusion = f32[64,32,256]{2,0,1:T(8,128)} fusion(f32[64,192]{1,0:T(8,128)S(1)} %fusion.41, f32[24,8,32,256]{3,2,1,0:T(8,128)} %bitcast.30), kind=kOutput, calls=%fused_computation | convolution fusion | flops 1207959552 | bytes 8437760 | tf_op jit(solution)/shard_map/dot_general | solution.py:75
  130.8 0.7 copy-done.4
  131.5 1.3 collective-permute-start.2
  132.8 4.5 %collective-permute-start = (s32[1,256]{1,0:T(1,128)S(1)}, s32[1,256]{1,0:T(1,128)S(1)}, u32[]{:S(2)}, u32[]{:S(2)}) collective-permute-start(s32[1,256]{1,0:T(1,128)S(1)} %get-tuple-element.34), channel_id=1, source_target_pairs={{0,1},{1,8},{8,9},{9,16},{16,17},{17,24},{24,25},{2,3},{3,10},{10,... | collective-permute-start | bytes 3080 | tf_op jit(solution)/shard_map/ppermute | solution.py:15
  137.3 0.1 constant_dynamic-slice_fusion
  137.4 0.6 copy.164
  138.0 0.6 collective-permute-done
  138.6 0.2 fusion.55
  138.8 10.2 %psum.23 = f32[64,64]{1,0:T(8,128)S(1)} all-reduce(f32[64,64]{1,0:T(8,128)S(1)} %fusion.55), channel_id=1, replica_groups=mesh['row'=4,'col'=4,'ch'=2] {'ch'}, use_global_device_ids=true, to_apply=%region_3.0 | all-reduce | flops 4096 | bytes 32768 | tf_op jit(solution)/shard_map/psum | solution.py:85
  149.0 13.5 %reduce-scatter.2.cloned.1.call-done = f32[64,16,256]{2,0,1:T(8,128)} async-done(((f32[64,32,256]{2,0,1:T(8,128)}), f32[64,16,256]{2,0,1:T(8,128)}) %reduce-scatter.2.cloned.1.call-update) | async-done | bytes 1048592 | tf_op jit(solution)/shard_map/reduce_scatter | solution.py:84
  162.5 1.3 copy.163
  163.8 1.1 fusion.5
  165.0 0.3 copy.166
  165.3 0.1 fusion.52
  165.4 1.3 collective-permute-start.3
  166.7 4.5 %collective-permute-start.1 = (f32[64,1,256]{2,0,1:T(8,128)S(1)}, f32[64,1,256]{2,0,1:T(8,128)S(1)}, u32[]{:S(2)}, u32[]{:S(2)}) collective-permute-start(f32[64,1,256]{2,0,1:T(8,128)S(1)} %copy.160), channel_id=1, source_target_pairs={{0,1},{1,8},{8,9},{9,16},{16,17},{17,24},{24,25},{2,3},{3,10},{10,... | collective-permute-start | bytes 196616 | tf_op jit(solution)/shard_map/ppermute | solution.py:15
  171.4 1.3 collective-permute-start.6
  172.7 3.0 %collective-permute-start.4 = (s32[18,1]{1,0:T(8,128)S(1)}, s32[18,1]{1,0:T(8,128)S(1)}, u32[]{:S(2)}, u32[]{:S(2)}) collective-permute-start(s32[18,1]{1,0:T(8,128)S(1)} %get-tuple-element.32), channel_id=1, source_target_pairs={{0,2},{2,4},{4,6},{1,3},{3,5},{5,7},{8,10},{10,12},{12,14},{9,11},... | collective-permute-start | bytes 224 | tf_op jit(solution)/shard_map/ppermute | solution.py:15
  175.7 1.6 copy.135
  177.3 0.1 copy.139
  177.4 0.1 copy.133
  177.5 3.0 %collective-permute-start.5 = (f32[64,18,1]{0,1,2:T(8,128)S(1)}, f32[64,18,1]{0,1,2:T(8,128)S(1)}, u32[]{:S(2)}, u32[]{:S(2)}) collective-permute-start(f32[64,18,1]{0,1,2:T(8,128)S(1)} %get-tuple-element.23), channel_id=1, source_target_pairs={{0,2},{2,4},{4,6},{1,3},{3,5},{5,7},{8,10},{10,12},{12,14},{9,11},... | collective-permute-start | bytes 13832 | tf_op jit(solution)/shard_map/ppermute | solution.py:15
  180.5 1.5 collective-permute-start.7
  182.1 0.1 add_add_fusion
  182.2 0.1 copy.145
  182.3 0.1 copy.131
  182.4 0.1 copy.136
  182.5 0.1 copy.140
  182.6 0.1 copy.144
  182.7 0.9 collective-permute-done.7
  183.6 9.2 %fusion.26 = f32[64,16,256]{0,1,2:T(8,128)S(1)} fusion(f32[64,18,1]{0,1,2:T(8,128)S(1)} %collective-permute-done.7, f32[64,1,256]{0,1,2:T(1,128)S(1)} %copy.139, f32[64,16,256]{0,1,2:T(8,128)} %copy-done.1, f32[64,1,256]{0,1,2:T(1,128)S(1)} %copy.133, f32[64,18,1]{0,1,2:T(8,128)S(1)} %collective-permute-done.5, f32[16,256]{0,1:T(8,128)S(1)} %copy.145, ...), kind=kLoop, calls=%fused_computation.44 | loop fusion | flops 4456448 | bytes 2319360 | tf_op jit(solution)/shard_map/div | solution.py:38
  192.8 0.2 fusion.51
  193.0 0.1 copy.148
  193.1 1.3 collective-permute-start.9
  194.4 0.1 copy.146
  194.5 4.5 %collective-permute-start.8 = (f32[64,1,256]{2,0,1:T(8,128)S(1)}, f32[64,1,256]{2,0,1:T(8,128)S(1)}, u32[]{:S(2)}, u32[]{:S(2)}) collective-permute-start(f32[64,1,256]{2,0,1:T(8,128)S(1)} %copy.146), channel_id=1, source_target_pairs={{0,1},{1,8},{8,9},{9,16},{16,17},{17,24},{24,25},{2,3},{3,10},{10,... | collective-permute-start | bytes 196616 | tf_op jit(solution)/shard_map/ppermute | solution.py:15
  199.0 0.2 collective-permute-done.9
  199.3 0.1 copy.149
  199.4 2.0 collective-permute-done.8
  201.3 0.1 copy.147
  201.4 2.8 collective-permute-start.10
  204.3 1.3 collective-permute-start.11
  205.6 2.4 collective-permute-done.11
  208.0 9.2 %fusion.17 = f32[64,16,256]{0,1,2:T(8,128)S(1)} fusion(f32[64,18,1]{0,1,2:T(8,128)S(1)} %collective-permute-done.11, f32[64,1,256]{0,1,2:T(1,128)S(1)} %copy.149, f32[64,16,256]{0,1,2:T(8,128)} %copy-done, f32[64,1,256]{0,1,2:T(1,128)S(1)} %copy.147, f32[64,18,1]{0,1,2:T(8,128)S(1)} %collective-permute-done.10, f32[16,256]{0,1:T(8,128)S(1)} %copy.145, ...), kind=kLoop, calls=%fused_computation.27 | loop fusion | flops 4456448 | bytes 2319360 | tf_op jit(solution)/shard_map/div | solution.py:38
  217.2 0.2 fusion.50
  217.5 1.3 collective-permute-start.13
  218.8 0.1 copy.152
  218.9 4.9 %collective-permute-start.12 = (f32[64,1,256]{2,0,1:T(8,128)S(1)}, f32[64,1,256]{2,0,1:T(8,128)S(1)}, u32[]{:S(2)}, u32[]{:S(2)}) collective-permute-start(f32[64,1,256]{2,0,1:T(8,128)S(1)} %copy.152), channel_id=1, source_target_pairs={{0,1},{1,8},{8,9},{9,16},{16,17},{17,24},{24,25},{2,3},{3,10},{10,... | collective-permute-start | bytes 196616 | tf_op jit(solution)/shard_map/ppermute | solution.py:15
  223.8 0.2 collective-permute-done.13
  224.0 0.1 copy.155
  224.1 1.6 collective-permute-done.12
  225.7 0.1 copy.153
  225.8 3.6 %collective-permute-start.14 = (f32[64,18,1]{0,1,2:T(8,128)S(1)}, f32[64,18,1]{0,1,2:T(8,128)S(1)}, u32[]{:S(2)}, u32[]{:S(2)}) collective-permute-start(f32[64,18,1]{0,1,2:T(8,128)S(1)} %get-tuple-element.19), channel_id=1, source_target_pairs={{0,2},{2,4},{4,6},{1,3},{3,5},{5,7},{8,10},{10,12},{12,14},{9,11},... | collective-permute-start | bytes 13832 | tf_op jit(solution)/shard_map/ppermute | solution.py:15
  229.4 1.3 collective-permute-start.15
  230.7 2.1 collective-permute-done.15
  232.7 5.2 %fusion.8 = f32[64,16,256]{0,1,2:T(8,128)} fusion(f32[64,18,1]{0,1,2:T(8,128)S(1)} %collective-permute-done.15, f32[64,1,256]{0,1,2:T(1,128)S(1)} %copy.155, f32[64,16,256]{0,1,2:T(8,128)S(1)} %fusion.17, f32[64,1,256]{0,1,2:T(1,128)S(1)} %copy.153, f32[64,18,1]{0,1,2:T(8,128)S(1)} %collective-permute-done.14, f32[16,256]{0,1:T(8,128)S(1)} %copy.145, ...), kind=kLoop, calls=%fused_computation.10 | loop fusion | flops 4456448 | bytes 2319360 | tf_op jit(solution)/shard_map/div | solution.py:38
  237.9 3.5 %copy.158 = f32[64,16,256]{2,0,1:T(8,128)} copy(f32[64,16,256]{0,1,2:T(8,128)} %fusion.8) | data formatting | bytes 2097152 | tf_op jit(solution)/shard_map/div | solution.py:38
  241.4 38.5 %all-gather.2.cloned.1.call-done = f32[64,32,256]{2,0,1:T(8,128)} async-done(((f32[64,16,256]{2,0,1:T(8,128)}), f32[64,32,256]{2,0,1:T(8,128)}) %all-gather.2.cloned.1.call-update) | async-done | bytes 2097168 | tf_op jit(solution)/shard_map/all_gather | solution.py:94
  280.0 4.1 %copy.159 = f32[64,32,256]{2,1,0:T(8,128)} copy(f32[64,32,256]{2,0,1:T(8,128)} %all-gather.2.cloned.1.call-done) | data formatting | bytes 4194304
  (34 shorter events, 0.4 us)
Async XLA Ops:
  7.2 7.1 %copy-start.2 = (f32[64,32,256]{2,1,0:T(8,128)S(1)}, f32[64,32,256]{2,1,0:T(8,128)}, u32[]{:S(2)}) copy-start(f32[64,32,256]{2,1,0:T(8,128)} %param.5) | copy-start | bytes 6291460
  7.2 111.1 %all-reduce.3.cloned.1.call-start = ((), (), s32[]{:S(2)}) async-start(), calls=%async_computation.3 | async-start | bytes 196608 | tf_op jit(solution)/shard_map/psum | solution.py:64
  14.2 104.0 %copy-start.5 = (f32[64,192]{1,0:T(8,128)S(1)}, f32[64,192]{1,0:T(8,128)}, u32[]{:S(2)}) copy-start(f32[64,192]{1,0:T(8,128)} %param.6) | copy-start | bytes 147460
  26.5 136.1 %reduce-scatter.2.cloned.1.call-start = ((), (), s32[]{:S(2)}) async-start(), calls=%async_computation.1 | async-start | bytes 3145728 | tf_op jit(solution)/shard_map/reduce_scatter | solution.py:84
  119.3 19.3 %copy-start.3 = (f32[64,192]{1,0:T(8,128)}, f32[64,192]{1,0:T(8,128)S(1)}, u32[]{:S(2)}) copy-start(f32[64,192]{1,0:T(8,128)S(1)} %fusion.41) | copy-start | bytes 147460
  130.7 0.8 copy-start.4
  130.7 149.3 %all-gather.2.cloned.1.call-start = ((), (), s32[]{:S(2)}) async-start(), calls=%async_computation.2 | async-start | bytes 3145728 | tf_op jit(solution)/shard_map/all_gather | solution.py:94
  131.5 6.6 %collective-permute-start.2 = (s32[1,256]{1,0:T(1,128)S(1)}, s32[1,256]{1,0:T(1,128)S(1)}, u32[]{:S(2)}, u32[]{:S(2)}) collective-permute-start(s32[1,256]{1,0:T(1,128)S(1)} %get-tuple-element.33), channel_id=1, source_target_pairs={{1,0},{8,1},{9,8},{16,9},{17,16},{24,17},{25,24},{3,2},{10,3},{11,... | collective-permute-start | bytes 3080 | tf_op jit(solution)/shard_map/ppermute | solution.py:18
  132.8 5.8 %collective-permute-start = (s32[1,256]{1,0:T(1,128)S(1)}, s32[1,256]{1,0:T(1,128)S(1)}, u32[]{:S(2)}, u32[]{:S(2)}) collective-permute-start(s32[1,256]{1,0:T(1,128)S(1)} %get-tuple-element.34), channel_id=1, source_target_pairs={{0,1},{1,8},{8,9},{9,16},{16,17},{17,24},{24,25},{2,3},{3,10},{10,... | collective-permute-start | bytes 3080 | tf_op jit(solution)/shard_map/ppermute | solution.py:15
  165.4 11.9 %collective-permute-start.3 = (f32[64,1,256]{2,0,1:T(8,128)S(1)}, f32[64,1,256]{2,0,1:T(8,128)S(1)}, u32[]{:S(2)}, u32[]{:S(2)}) collective-permute-start(f32[64,1,256]{2,0,1:T(8,128)S(1)} %copy.161), channel_id=1, source_target_pairs={{1,0},{8,1},{9,8},{16,9},{17,16},{24,17},{25,24},{3,2},{10,3},{11,... | collective-permute-start | bytes 196616 | tf_op jit(solution)/shard_map/ppermute | solution.py:18
  166.7 10.7 %collective-permute-start.1 = (f32[64,1,256]{2,0,1:T(8,128)S(1)}, f32[64,1,256]{2,0,1:T(8,128)S(1)}, u32[]{:S(2)}, u32[]{:S(2)}) collective-permute-start(f32[64,1,256]{2,0,1:T(8,128)S(1)} %copy.160), channel_id=1, source_target_pairs={{0,1},{1,8},{8,9},{9,16},{16,17},{17,24},{24,25},{2,3},{3,10},{10,... | collective-permute-start | bytes 196616 | tf_op jit(solution)/shard_map/ppermute | solution.py:15
  171.4 10.7 %collective-permute-start.6 = (s32[18,1]{1,0:T(8,128)S(1)}, s32[18,1]{1,0:T(8,128)S(1)}, u32[]{:S(2)}, u32[]{:S(2)}) collective-permute-start(s32[18,1]{1,0:T(8,128)S(1)} %get-tuple-element.31), channel_id=1, source_target_pairs={{2,0},{4,2},{6,4},{3,1},{5,3},{7,5},{10,8},{12,10},{14,12},{11,9},... | collective-permute-start | bytes 224 | tf_op jit(solution)/shard_map/ppermute | solution.py:18
  172.7 9.4 %collective-permute-start.4 = (s32[18,1]{1,0:T(8,128)S(1)}, s32[18,1]{1,0:T(8,128)S(1)}, u32[]{:S(2)}, u32[]{:S(2)}) collective-permute-start(s32[18,1]{1,0:T(8,128)S(1)} %get-tuple-element.32), channel_id=1, source_target_pairs={{0,2},{2,4},{4,6},{1,3},{3,5},{5,7},{8,10},{10,12},{12,14},{9,11},... | collective-permute-start | bytes 224 | tf_op jit(solution)/shard_map/ppermute | solution.py:15
  177.3 5.4 %copy-start.1 = (f32[64,16,256]{0,1,2:T(8,128)}, f32[64,16,256]{0,1,2:T(8,128)S(1)}, u32[]{:S(2)}) copy-start(f32[64,16,256]{0,1,2:T(8,128)S(1)} %copy.135) | copy-start | bytes 3145732
  177.5 5.1 %collective-permute-start.5 = (f32[64,18,1]{0,1,2:T(8,128)S(1)}, f32[64,18,1]{0,1,2:T(8,128)S(1)}, u32[]{:S(2)}, u32[]{:S(2)}) collective-permute-start(f32[64,18,1]{0,1,2:T(8,128)S(1)} %get-tuple-element.23), channel_id=1, source_target_pairs={{0,2},{2,4},{4,6},{1,3},{3,5},{5,7},{8,10},{10,12},{12,14},{9,11},... | collective-permute-start | bytes 13832 | tf_op jit(solution)/shard_map/ppermute | solution.py:15
  180.5 3.1 %collective-permute-start.7 = (f32[64,18,1]{0,1,2:T(8,128)S(1)}, f32[64,18,1]{0,1,2:T(8,128)S(1)}, u32[]{:S(2)}, u32[]{:S(2)}) collective-permute-start(f32[64,18,1]{0,1,2:T(8,128)S(1)} %get-tuple-element.24), channel_id=1, source_target_pairs={{2,0},{4,2},{6,4},{3,1},{5,3},{7,5},{10,8},{12,10},{14,12},{11,9},... | collective-permute-start | bytes 13832 | tf_op jit(solution)/shard_map/ppermute | solution.py:18
  192.8 12.8 %copy-start = (f32[64,16,256]{0,1,2:T(8,128)}, f32[64,16,256]{0,1,2:T(8,128)S(1)}, u32[]{:S(2)}) copy-start(f32[64,16,256]{0,1,2:T(8,128)S(1)} %fusion.26) | copy-start | bytes 3145732
  193.1 6.2 %collective-permute-start.9 = (f32[64,1,256]{2,0,1:T(8,128)S(1)}, f32[64,1,256]{2,0,1:T(8,128)S(1)}, u32[]{:S(2)}, u32[]{:S(2)}) collective-permute-start(f32[64,1,256]{2,0,1:T(8,128)S(1)} %copy.148), channel_id=1, source_target_pairs={{1,0},{8,1},{9,8},{16,9},{17,16},{24,17},{25,24},{3,2},{10,3},{11,... | collective-permute-start | bytes 196616 | tf_op jit(solution)/shard_map/ppermute | solution.py:18
  194.5 6.8 %collective-permute-start.8 = (f32[64,1,256]{2,0,1:T(8,128)S(1)}, f32[64,1,256]{2,0,1:T(8,128)S(1)}, u32[]{:S(2)}, u32[]{:S(2)}) collective-permute-start(f32[64,1,256]{2,0,1:T(8,128)S(1)} %copy.146), channel_id=1, source_target_pairs={{0,1},{1,8},{8,9},{9,16},{16,17},{17,24},{24,25},{2,3},{3,10},{10,... | collective-permute-start | bytes 196616 | tf_op jit(solution)/shard_map/ppermute | solution.py:15
  201.4 4.1 %collective-permute-start.10 = (f32[64,18,1]{0,1,2:T(8,128)S(1)}, f32[64,18,1]{0,1,2:T(8,128)S(1)}, u32[]{:S(2)}, u32[]{:S(2)}) collective-permute-start(f32[64,18,1]{0,1,2:T(8,128)S(1)} %get-tuple-element.21), channel_id=1, source_target_pairs={{0,2},{2,4},{4,6},{1,3},{3,5},{5,7},{8,10},{10,12},{12,14},{9,11},... | collective-permute-start | bytes 13832 | tf_op jit(solution)/shard_map/ppermute | solution.py:15
  204.3 3.7 %collective-permute-start.11 = (f32[64,18,1]{0,1,2:T(8,128)S(1)}, f32[64,18,1]{0,1,2:T(8,128)S(1)}, u32[]{:S(2)}, u32[]{:S(2)}) collective-permute-start(f32[64,18,1]{0,1,2:T(8,128)S(1)} %get-tuple-element.22), channel_id=1, source_target_pairs={{2,0},{4,2},{6,4},{3,1},{5,3},{7,5},{10,8},{12,10},{14,12},{11,9},... | collective-permute-start | bytes 13832 | tf_op jit(solution)/shard_map/ppermute | solution.py:18
  217.5 6.5 %collective-permute-start.13 = (f32[64,1,256]{2,0,1:T(8,128)S(1)}, f32[64,1,256]{2,0,1:T(8,128)S(1)}, u32[]{:S(2)}, u32[]{:S(2)}) collective-permute-start(f32[64,1,256]{2,0,1:T(8,128)S(1)} %copy.154), channel_id=1, source_target_pairs={{1,0},{8,1},{9,8},{16,9},{17,16},{24,17},{25,24},{3,2},{10,3},{11,... | collective-permute-start | bytes 196616 | tf_op jit(solution)/shard_map/ppermute | solution.py:18
  218.9 6.8 %collective-permute-start.12 = (f32[64,1,256]{2,0,1:T(8,128)S(1)}, f32[64,1,256]{2,0,1:T(8,128)S(1)}, u32[]{:S(2)}, u32[]{:S(2)}) collective-permute-start(f32[64,1,256]{2,0,1:T(8,128)S(1)} %copy.152), channel_id=1, source_target_pairs={{0,1},{1,8},{8,9},{9,16},{16,17},{17,24},{24,25},{2,3},{3,10},{10,... | collective-permute-start | bytes 196616 | tf_op jit(solution)/shard_map/ppermute | solution.py:15
  225.8 4.9 %collective-permute-start.14 = (f32[64,18,1]{0,1,2:T(8,128)S(1)}, f32[64,18,1]{0,1,2:T(8,128)S(1)}, u32[]{:S(2)}, u32[]{:S(2)}) collective-permute-start(f32[64,18,1]{0,1,2:T(8,128)S(1)} %get-tuple-element.19), channel_id=1, source_target_pairs={{0,2},{2,4},{4,6},{1,3},{3,5},{5,7},{8,10},{10,12},{12,14},{9,11},... | collective-permute-start | bytes 13832 | tf_op jit(solution)/shard_map/ppermute | solution.py:15
  229.4 3.4 %collective-permute-start.15 = (f32[64,18,1]{0,1,2:T(8,128)S(1)}, f32[64,18,1]{0,1,2:T(8,128)S(1)}, u32[]{:S(2)}, u32[]{:S(2)}) collective-permute-start(f32[64,18,1]{0,1,2:T(8,128)S(1)} %get-tuple-element.20), channel_id=1, source_target_pairs={{2,0},{4,2},{6,4},{3,1},{5,3},{7,5},{10,8},{12,10},{14,12},{11,9},... | collective-permute-start | bytes 13832 | tf_op jit(solution)/shard_map/ppermute | solution.py:18
Sparse Core Ops, SparseCore 0:
  26.6 91.6 all-reduce.2
  130.8 31.6 reduce-scatter.1
  241.6 38.3 all-gather.1
where the time goes:
time: 292 us; the launch traced here: 291 us
  waiting for transfers between devices  154 us (53%)
  starting transfers between devices  41.8 us (14%)
  matrix products  33 us (11%)
  other arithmetic  23.7 us (8%)
  between operations  14.2 us (5%)
  local copies, waits for them, and re-layouts  14.1 us (5%)
  blocking collectives  10.2 us (3%)
    psum x1, waiting for transfers between devices, shards(): chan_top, pixel_gram = lax.psum((chan_top, pixel_gram), ('row', 'col'))  91.5 us
    all_gather x1, waiting for transfers between devices, shards(): smoothed_factor = lax.all_gather(field, 'ch', axis=1, tiled=True)  38.5 us
    ppermute x8, starting transfers between devices, padded_2(): lax.ppermute(lax.slice_in_dim(block, block.shape[dim] - width, None, axis...  31 us
    div x3, other arithmetic, smooth_once(): return combined / (1.0 + weights[0] + weights[1] + weights[2] + weights[3])  23.6 us
    reduce_scatter x1, waiting for transfers between devices, shards(): lax.psum_scatter(part_top, 'ch', scatter_dimension=1, tiled=True)  13.5 us
    dot_general x1, matrix products, shards(): lax.dot_general(flat_pixel, flat_data, contraction, precision=precise, pr...  12.2 us
    dot_general x1, matrix products, shards(): jnp.dot(new_channel, flat_data, precision=precise, preferred_element_type...  11.4 us
    ppermute x8, starting transfers between devices, padded_2(): lax.ppermute(lax.slice_in_dim(block, 0, width, axis=dim), axis, backward)  10.5 us
  transfers between devices with their start and end apart: 19, of which 11 were waited for; matrix products, arithmetic and copies ran while one was open for 1% of the time, Pallas kernels for 0%

commit v1 on v0

--- a/solution.py
+++ b/solution.py
@@ -91,7 +91,8 @@
     for iteration in range(SMOOTH):
         padded = padded_2(field, ((("row", "ch"), 1), ("col", 2)), 1)
         field = smooth_once(padded, field, weights)
-    smoothed_factor = lax.all_gather(field, "ch", axis=1, tiled=True)
+    tiles = lax.all_gather(field, "ch")
+    smoothed_factor = jnp.concatenate(tiles, axis=1)
     return (smoothed_factor, new_channel)
 
 

time: 292 us -> 279 us (0.955)
  other arithmetic: 23.7 us -> 14.7 us
  waiting for transfers between devices: 154 us -> 161 us
  local copies, waits for them, and re-layouts: 14.1 us -> 8.37 us
  starting transfers between devices: 41.8 us -> 36.6 us
    ppermute x8, waiting for transfers between devices: 5.83 us -> 19.3 us  [padded_2(): lax.ppermute(lax.slice_in_dim(block, 0, width, axis=dim), axis, backward)]
    div x3, other arithmetic: 23.6 us -> 14.5 us  [smooth_once(): return combined / (1.0 + weights[0] + weights[1] + weights[2] + weights[3])]
    ppermute x8, starting transfers between devices: 31 us -> 26 us  [padded_2(): lax.ppermute(lax.slice_in_dim(block, block.shape[dim] - width, None, axis...]
    all_gather x1, waiting for transfers between devices: 38.5 us -> 33.8 us  [shards(): tiles = lax.all_gather(field, 'ch')]
    unnamed x17 -> x9, local copies, waits for them, and re-layouts: 5.77 us -> 1.3 us
    reshape x0 -> x1, local copies, waits for them, and re-layouts: none -> 3.15 us  [shards(): smoothed_factor = jnp.concatenate(tiles, axis=1)]
  transfers between devices with their start and end apart: 19 -> 19, of which waited for: 11 -> 12; matrix products, arithmetic and copies ran while one was open for 1% -> 0% of each run, Pallas kernels for 0% -> 0%
where the time goes in v1:
time: 279 us; the launch traced here: 278 us
  waiting for transfers between devices  161 us (58%)
  starting transfers between devices  36.6 us (13%)
  matrix products  33 us (12%)
  other arithmetic  14.7 us (5%)
  between operations  14.1 us (5%)
  blocking collectives  10.2 us (4%)
  local copies, waits for them, and re-layouts  8.37 us (3%)
    psum x1, waiting for transfers between devices, shards(): chan_top, pixel_gram = lax.psum((chan_top, pixel_gram), ('row', 'col'))  91.5 us
    all_gather x1, waiting for transfers between devices, shards(): tiles = lax.all_gather(field, 'ch')  33.8 us
    ppermute x8, starting transfers between devices, padded_2(): lax.ppermute(lax.slice_in_dim(block, block.shape[dim] - width, None, axis...  26 us
    ppermute x8, waiting for transfers between devices, padded_2(): lax.ppermute(lax.slice_in_dim(block, 0, width, axis=dim), axis, backward)  19.3 us
    div x3, other arithmetic, smooth_once(): return combined / (1.0 + weights[0] + weights[1] + weights[2] + weights[3])  14.5 us
    reduce_scatter x1, waiting for transfers between devices, shards(): lax.psum_scatter(part_top, 'ch', scatter_dimension=1, tiled=True)  13.5 us
    dot_general x1, matrix products, shards(): lax.dot_general(flat_pixel, flat_data, contraction, precision=precise, pr...  12.2 us
    dot_general x1, matrix products, shards(): jnp.dot(new_channel, flat_data, precision=precise, preferred_element_type...  11.4 us
  transfers between devices with their start and end apart: 19, of which 12 were waited for; matrix products, arithmetic and copies ran while one was open for 0% of the time, Pallas kernels for 0%

profile of v1, /device:TPU:0, one launch (start us, length us, event | category | flops | bytes accessed | tf_op | source)
XLA Modules:
  0.0 278.1 jit_solution(4968628495983692188)
XLA Ops:
  7.2 0.0 copy-start
  7.2 0.0 all-reduce.3.cloned.1.call-start
  7.2 7.0 %fusion.42 = f32[64,64]{1,0:T(8,128)} fusion(f32[64,32,256]{2,1,0:T(8,128)} %param.5), kind=kOutput, calls=%fused_computation.64 | convolution fusion | flops 402653184 | bytes 2113536 | tf_op jit(solution)/shard_map/dot_general | solution.py:61
  14.2 0.0 copy-done
  14.2 12.2 %fusion.36 = f32[64,192]{1,0:T(8,128)} fusion(f32[192,32,256]{2,1,0:T(8,128)} %param.4, f32[64,32,256]{2,1,0:T(8,128)S(1)} %copy-done), kind=kOutput, calls=%fused_computation.61 | convolution fusion | flops 1207959552 | bytes 8437760 | tf_op jit(solution)/shard_map/dot_general | solution.py:58
  26.4 0.0 all-reduce.3.cloned.1.call-update
  26.5 0.2 reduce-scatter.2.cloned.1.call-start
  26.7 91.5 %all-reduce.3.cloned.1.call-done = (f32[64,64]{1,0:T(8,128)}, f32[64,192]{1,0:T(8,128)}) async-done(((f32[64,64]{1,0:T(8,128)}, f32[64,192]{1,0:T(8,128)}), (f32[64,64]{1,0:T(8,128)}, f32[64,192]{1,0:T(8,128)})) %all-reduce.3.cloned.1.call-update) | async-done | bytes 65552 | tf_op jit(solution)/shard_map/psum | solution.py:64
  118.2 0.0 copy-done.3
  118.2 1.1 fusion.41
  119.3 0.0 copy-start.1
  119.3 11.4 %fusion = f32[64,32,256]{2,0,1:T(8,128)} fusion(f32[64,192]{1,0:T(8,128)S(1)} %fusion.41, f32[24,8,32,256]{3,2,1,0:T(8,128)} %bitcast.33), kind=kOutput, calls=%fused_computation | convolution fusion | flops 1207959552 | bytes 8437760 | tf_op jit(solution)/shard_map/dot_general | solution.py:75
  130.7 0.0 reduce-scatter.2.cloned.1.call-update
  130.7 0.0 all-gather.3.cloned.1.call-start
  130.8 0.7 copy-done.2
  131.5 1.3 collective-permute-start.2
  132.8 4.5 %collective-permute-start = (s32[1,256]{1,0:T(1,128)S(1)}, s32[1,256]{1,0:T(1,128)S(1)}, u32[]{:S(2)}, u32[]{:S(2)}) collective-permute-start(s32[1,256]{1,0:T(1,128)S(1)} %get-tuple-element.24), channel_id=1, source_target_pairs={{0,1},{1,8},{8,9},{9,16},{16,17},{17,24},{24,25},{2,3},{3,10},{10,... | collective-permute-start | bytes 3080 | tf_op jit(solution)/shard_map/ppermute | solution.py:15
  137.3 0.1 constant_dynamic-slice_fusion
  137.4 0.6 copy.31
  138.0 0.0 collective-permute-done.2
  138.0 0.6 collective-permute-done
  138.6 0.2 fusion.55
  138.8 10.2 %psum.23 = f32[64,64]{1,0:T(8,128)S(1)} all-reduce(f32[64,64]{1,0:T(8,128)S(1)} %fusion.55), channel_id=1, replica_groups=mesh['row'=4,'col'=4,'ch'=2] {'ch'}, use_global_device_ids=true, to_apply=%region_3.0 | all-reduce | flops 4096 | bytes 32768 | tf_op jit(solution)/shard_map/psum | solution.py:85
  149.0 13.5 %reduce-scatter.2.cloned.1.call-done = f32[64,16,256]{2,0,1:T(8,128)} async-done(((f32[64,32,256]{2,0,1:T(8,128)}), f32[64,16,256]{2,0,1:T(8,128)}) %reduce-scatter.2.cloned.1.call-update) | async-done | bytes 1048592 | tf_op jit(solution)/shard_map/reduce_scatter | solution.py:84
  162.5 1.3 copy.30
  163.8 1.1 fusion.5
  165.0 0.6 copy.28
  165.6 2.3 collective-permute-start.1
  167.9 1.3 collective-permute-start.3
  169.2 0.1 fusion.53
  169.3 1.3 collective-permute-start.6
  170.6 3.0 %collective-permute-start.4 = (s32[18,1]{1,0:T(8,128)S(1)}, s32[18,1]{1,0:T(8,128)S(1)}, u32[]{:S(2)}, u32[]{:S(2)}) collective-permute-start(s32[18,1]{1,0:T(8,128)S(1)} %get-tuple-element.22), channel_id=1, source_target_pairs={{0,2},{2,4},{4,6},{1,3},{3,5},{5,7},{8,10},{10,12},{12,14},{9,11},... | collective-permute-start | bytes 224 | tf_op jit(solution)/shard_map/ppermute | solution.py:15
  173.6 0.0 collective-permute-done.1
  173.6 1.8 collective-permute-done.3
  175.5 1.4 collective-permute-start.5
  176.9 1.3 collective-permute-start.7
  178.2 0.0 collective-permute-done.6
  178.2 0.0 collective-permute-done.4
  178.2 0.1 add_add_fusion
  178.3 0.0 collective-permute-done.5
  178.3 3.3 %collective-permute-done.7 = f32[64,18,1]{0,2,1:T(1,128)S(1)} collective-permute-done((f32[64,18,1]{0,2,1:T(1,128)S(1)}, f32[64,18,1]{0,2,1:T(1,128)S(1)}, u32[]{:S(2)}, u32[]{:S(2)}) %collective-permute-start.7) | collective-permute-done | bytes 4640 | tf_op jit(solution)/shard_map/ppermute | solution.py:18
  181.6 4.8 %fusion.26 = f32[64,16,256]{0,2,1:T(8,128)S(1)} fusion(f32[64,18,1]{0,2,1:T(1,128)S(1)} %collective-permute-done.7, f32[64,1,256]{0,2,1:T(8,128)S(1)} %collective-permute-done.3, f32[64,16,256]{0,2,1:T(8,128)S(1)} %bitcast.36, f32[64,1,256]{0,2,1:T(8,128)S(1)} %collective-permute-done.1, f32[64,18,1]{0,2,1:T(1,128)S(1)} %collective-permute-done.5, ...), kind=kLoop, calls=%fused_computation.44 | loop fusion | flops 4456448 | bytes 2319360 | tf_op jit(solution)/shard_map/div | solution.py:38
  186.4 4.7 %collective-permute-start.8 = (f32[64,1,256]{0,2,1:T(8,128)S(1)}, f32[64,1,256]{0,2,1:T(8,128)S(1)}, u32[]{:S(2)}, u32[]{:S(2)}) collective-permute-start(f32[64,1,256]{0,2,1:T(8,128)S(1)} %get-tuple-element.17), channel_id=1, source_target_pairs={{0,1},{1,8},{8,9},{9,16},{16,17},{17,24},{24,25},{2,3},{3,10},{10,... | collective-permute-start | bytes 196616 | tf_op jit(solution)/shard_map/ppermute | solution.py:15
  191.1 1.3 collective-permute-start.9
  192.4 1.2 collective-permute-done.8
  193.6 4.6 %collective-permute-done.9 = f32[64,1,256]{0,2,1:T(8,128)S(1)} collective-permute-done((f32[64,1,256]{0,2,1:T(8,128)S(1)}, f32[64,1,256]{0,2,1:T(8,128)S(1)}, u32[]{:S(2)}, u32[]{:S(2)}) %collective-permute-start.9) | collective-permute-done | bytes 65568 | tf_op jit(solution)/shard_map/ppermute | solution.py:18
  198.3 2.9 %collective-permute-start.10 = (f32[64,18,1]{0,2,1:T(1,128)S(1)}, f32[64,18,1]{0,2,1:T(1,128)S(1)}, u32[]{:S(2)}, u32[]{:S(2)}) collective-permute-start(f32[64,18,1]{0,2,1:T(1,128)S(1)} %get-tuple-element.11), channel_id=1, source_target_pairs={{0,2},{2,4},{4,6},{1,3},{3,5},{5,7},{8,10},{10,12},{12,14},{9,11},... | collective-permute-start | bytes 13832 | tf_op jit(solution)/shard_map/ppermute | solution.py:15
  201.2 1.3 collective-permute-start.11
  202.5 0.0 collective-permute-done.10
  202.5 2.5 collective-permute-done.11
  204.9 4.8 %fusion.17 = f32[64,16,256]{0,2,1:T(8,128)S(1)} fusion(f32[64,18,1]{0,2,1:T(1,128)S(1)} %collective-permute-done.11, f32[64,1,256]{0,2,1:T(8,128)S(1)} %collective-permute-done.9, f32[64,16,256]{0,2,1:T(8,128)S(1)} %fusion.26, f32[64,1,256]{0,2,1:T(8,128)S(1)} %collective-permute-done.8, f32[64,18,1]{0,2,1:T(1,128)S(1)} %collective-permute-done.10, ...), kind=kLoop, calls=%fused_computation.27 | loop fusion | flops 4456448 | bytes 2319360 | tf_op jit(solution)/shard_map/div | solution.py:38
  209.8 4.3 %collective-permute-start.12 = (f32[64,1,256]{0,2,1:T(8,128)S(1)}, f32[64,1,256]{0,2,1:T(8,128)S(1)}, u32[]{:S(2)}, u32[]{:S(2)}) collective-permute-start(f32[64,1,256]{0,2,1:T(8,128)S(1)} %get-tuple-element.15), channel_id=1, source_target_pairs={{0,1},{1,8},{8,9},{9,16},{16,17},{17,24},{24,25},{2,3},{3,10},{10,... | collective-permute-start | bytes 196616 | tf_op jit(solution)/shard_map/ppermute | solution.py:15
  214.1 1.3 collective-permute-start.13
  215.4 1.2 collective-permute-done.12
  216.6 4.6 %collective-permute-done.13 = f32[64,1,256]{0,2,1:T(8,128)S(1)} collective-permute-done((f32[64,1,256]{0,2,1:T(8,128)S(1)}, f32[64,1,256]{0,2,1:T(8,128)S(1)}, u32[]{:S(2)}, u32[]{:S(2)}) %collective-permute-start.13) | collective-permute-done | bytes 65568 | tf_op jit(solution)/shard_map/ppermute | solution.py:18
  221.3 2.9 %collective-permute-start.14 = (f32[64,18,1]{0,2,1:T(1,128)S(1)}, f32[64,18,1]{0,2,1:T(1,128)S(1)}, u32[]{:S(2)}, u32[]{:S(2)}) collective-permute-start(f32[64,18,1]{0,2,1:T(1,128)S(1)} %get-tuple-element.9), channel_id=1, source_target_pairs={{0,2},{2,4},{4,6},{1,3},{3,5},{5,7},{8,10},{10,12},{12,14},{9,11},... | collective-permute-start | bytes 13832 | tf_op jit(solution)/shard_map/ppermute | solution.py:15
  224.2 1.3 collective-permute-start.15
  225.5 0.0 collective-permute-done.14
  225.5 2.5 collective-permute-done.15
  228.0 4.8 %fusion.8 = f32[64,16,256]{0,2,1:T(8,128)S(1)} fusion(f32[64,18,1]{0,2,1:T(1,128)S(1)} %collective-permute-done.15, f32[64,1,256]{0,2,1:T(8,128)S(1)} %collective-permute-done.13, f32[64,16,256]{0,2,1:T(8,128)S(1)} %fusion.17, f32[64,1,256]{0,2,1:T(8,128)S(1)} %collective-permute-done.12, f32[64,18,1]{0,2,1:T(1,128)S(1)} %collective-permute-done.14, ...), kind=kLoop, calls=%fused_computation.10 | loop fusion | flops 4456448 | bytes 2319360 | tf_op jit(solution)/shard_map/div | solution.py:38
  232.8 1.8 copy.26
  234.6 0.0 all-gather.3.cloned.1.call-update
  234.6 33.8 %all-gather.3.cloned.1.call-done = f32[128,16,256]{2,1,0:T(8,128)} async-done(((f32[64,16,256]{2,1,0:T(8,128)}), f32[128,16,256]{2,1,0:T(8,128)}) %all-gather.3.cloned.1.call-update) | async-done | bytes 2097168 | tf_op jit(solution)/shard_map/all_gather | solution.py:94
  268.4 3.2 %copy.27 = f32[64,2,16,256]{3,2,1,0:T(8,128)} copy(f32[64,2,16,256]{3,2,0,1:T(8,128)} %bitcast.38) | data formatting | bytes 4194304 | tf_op jit(solution)/shard_map/reshape | solution.py:95
  (12 shorter events, 0.1 us)
Async XLA Ops:
  7.2 7.1 %copy-start = (f32[64,32,256]{2,1,0:T(8,128)S(1)}, f32[64,32,256]{2,1,0:T(8,128)}, u32[]{:S(2)}) copy-start(f32[64,32,256]{2,1,0:T(8,128)} %param.5) | copy-start | bytes 6291460
  7.2 111.1 %all-reduce.3.cloned.1.call-start = ((), (), s32[]{:S(2)}) async-start(), calls=%async_computation.3 | async-start | bytes 196608 | tf_op jit(solution)/shard_map/psum | solution.py:64
  14.2 104.0 %copy-start.3 = (f32[64,192]{1,0:T(8,128)S(1)}, f32[64,192]{1,0:T(8,128)}, u32[]{:S(2)}) copy-start(f32[64,192]{1,0:T(8,128)} %param.6) | copy-start | bytes 147460
  26.5 136.1 %reduce-scatter.2.cloned.1.call-start = ((), (), s32[]{:S(2)}) async-start(), calls=%async_computation.1 | async-start | bytes 3145728 | tf_op jit(solution)/shard_map/reduce_scatter | solution.py:84
  119.3 19.3 %copy-start.1 = (f32[64,192]{1,0:T(8,128)}, f32[64,192]{1,0:T(8,128)S(1)}, u32[]{:S(2)}) copy-start(f32[64,192]{1,0:T(8,128)S(1)} %fusion.41) | copy-start | bytes 147460
  130.7 0.8 copy-start.2
  130.7 137.7 %all-gather.3.cloned.1.call-start = ((), (), s32[]{:S(2)}) async-start(), calls=%async_computation.2 | async-start | bytes 3145728 | tf_op jit(solution)/shard_map/all_gather | solution.py:94
  131.5 6.6 %collective-permute-start.2 = (s32[1,256]{1,0:T(1,128)S(1)}, s32[1,256]{1,0:T(1,128)S(1)}, u32[]{:S(2)}, u32[]{:S(2)}) collective-permute-start(s32[1,256]{1,0:T(1,128)S(1)} %get-tuple-element.23), channel_id=1, source_target_pairs={{1,0},{8,1},{9,8},{16,9},{17,16},{24,17},{25,24},{3,2},{10,3},{11,... | collective-permute-start | bytes 3080 | tf_op jit(solution)/shard_map/ppermute | solution.py:18
  132.8 5.8 %collective-permute-start = (s32[1,256]{1,0:T(1,128)S(1)}, s32[1,256]{1,0:T(1,128)S(1)}, u32[]{:S(2)}, u32[]{:S(2)}) collective-permute-start(s32[1,256]{1,0:T(1,128)S(1)} %get-tuple-element.24), channel_id=1, source_target_pairs={{0,1},{1,8},{8,9},{9,16},{16,17},{17,24},{24,25},{2,3},{3,10},{10,... | collective-permute-start | bytes 3080 | tf_op jit(solution)/shard_map/ppermute | solution.py:15
  165.6 8.0 %collective-permute-start.1 = (f32[64,1,256]{0,2,1:T(8,128)S(1)}, f32[64,1,256]{0,2,1:T(8,128)S(1)}, u32[]{:S(2)}, u32[]{:S(2)}) collective-permute-start(f32[64,1,256]{0,2,1:T(8,128)S(1)} %get-tuple-element.19), channel_id=1, source_target_pairs={{0,1},{1,8},{8,9},{9,16},{16,17},{17,24},{24,25},{2,3},{3,10},{10,... | collective-permute-start | bytes 196616 | tf_op jit(solution)/shard_map/ppermute | solution.py:15
  167.9 7.6 %collective-permute-start.3 = (f32[64,1,256]{0,2,1:T(8,128)S(1)}, f32[64,1,256]{0,2,1:T(8,128)S(1)}, u32[]{:S(2)}, u32[]{:S(2)}) collective-permute-start(f32[64,1,256]{0,2,1:T(8,128)S(1)} %get-tuple-element.20), channel_id=1, source_target_pairs={{1,0},{8,1},{9,8},{16,9},{17,16},{24,17},{25,24},{3,2},{10,3},{11,... | collective-permute-start | bytes 196616 | tf_op jit(solution)/shard_map/ppermute | solution.py:18
  169.3 8.9 %collective-permute-start.6 = (s32[18,1]{1,0:T(8,128)S(1)}, s32[18,1]{1,0:T(8,128)S(1)}, u32[]{:S(2)}, u32[]{:S(2)}) collective-permute-start(s32[18,1]{1,0:T(8,128)S(1)} %get-tuple-element.21), channel_id=1, source_target_pairs={{2,0},{4,2},{6,4},{3,1},{5,3},{7,5},{10,8},{12,10},{14,12},{11,9},... | collective-permute-start | bytes 224 | tf_op jit(solution)/shard_map/ppermute | solution.py:18
  170.6 7.6 %collective-permute-start.4 = (s32[18,1]{1,0:T(8,128)S(1)}, s32[18,1]{1,0:T(8,128)S(1)}, u32[]{:S(2)}, u32[]{:S(2)}) collective-permute-start(s32[18,1]{1,0:T(8,128)S(1)} %get-tuple-element.22), channel_id=1, source_target_pairs={{0,2},{2,4},{4,6},{1,3},{3,5},{5,7},{8,10},{10,12},{12,14},{9,11},... | collective-permute-start | bytes 224 | tf_op jit(solution)/shard_map/ppermute | solution.py:15
  175.5 2.8 %collective-permute-start.5 = (f32[64,18,1]{0,2,1:T(1,128)S(1)}, f32[64,18,1]{0,2,1:T(1,128)S(1)}, u32[]{:S(2)}, u32[]{:S(2)}) collective-permute-start(f32[64,18,1]{0,2,1:T(1,128)S(1)} %get-tuple-element.13), channel_id=1, source_target_pairs={{0,2},{2,4},{4,6},{1,3},{3,5},{5,7},{8,10},{10,12},{12,14},{9,11},... | collective-permute-start | bytes 13832 | tf_op jit(solution)/shard_map/ppermute | solution.py:15
  176.9 4.7 %collective-permute-start.7 = (f32[64,18,1]{0,2,1:T(1,128)S(1)}, f32[64,18,1]{0,2,1:T(1,128)S(1)}, u32[]{:S(2)}, u32[]{:S(2)}) collective-permute-start(f32[64,18,1]{0,2,1:T(1,128)S(1)} %get-tuple-element.14), channel_id=1, source_target_pairs={{2,0},{4,2},{6,4},{3,1},{5,3},{7,5},{10,8},{12,10},{14,12},{11,9},... | collective-permute-start | bytes 13832 | tf_op jit(solution)/shard_map/ppermute | solution.py:18
  186.4 7.2 %collective-permute-start.8 = (f32[64,1,256]{0,2,1:T(8,128)S(1)}, f32[64,1,256]{0,2,1:T(8,128)S(1)}, u32[]{:S(2)}, u32[]{:S(2)}) collective-permute-start(f32[64,1,256]{0,2,1:T(8,128)S(1)} %get-tuple-element.17), channel_id=1, source_target_pairs={{0,1},{1,8},{8,9},{9,16},{16,17},{17,24},{24,25},{2,3},{3,10},{10,... | collective-permute-start | bytes 196616 | tf_op jit(solution)/shard_map/ppermute | solution.py:15
  191.1 7.1 %collective-permute-start.9 = (f32[64,1,256]{0,2,1:T(8,128)S(1)}, f32[64,1,256]{0,2,1:T(8,128)S(1)}, u32[]{:S(2)}, u32[]{:S(2)}) collective-permute-start(f32[64,1,256]{0,2,1:T(8,128)S(1)} %get-tuple-element.18), channel_id=1, source_target_pairs={{1,0},{8,1},{9,8},{16,9},{17,16},{24,17},{25,24},{3,2},{10,3},{11,... | collective-permute-start | bytes 196616 | tf_op jit(solution)/shard_map/ppermute | solution.py:18
  198.3 4.2 %collective-permute-start.10 = (f32[64,18,1]{0,2,1:T(1,128)S(1)}, f32[64,18,1]{0,2,1:T(1,128)S(1)}, u32[]{:S(2)}, u32[]{:S(2)}) collective-permute-start(f32[64,18,1]{0,2,1:T(1,128)S(1)} %get-tuple-element.11), channel_id=1, source_target_pairs={{0,2},{2,4},{4,6},{1,3},{3,5},{5,7},{8,10},{10,12},{12,14},{9,11},... | collective-permute-start | bytes 13832 | tf_op jit(solution)/shard_map/ppermute | solution.py:15
  201.2 3.8 %collective-permute-start.11 = (f32[64,18,1]{0,2,1:T(1,128)S(1)}, f32[64,18,1]{0,2,1:T(1,128)S(1)}, u32[]{:S(2)}, u32[]{:S(2)}) collective-permute-start(f32[64,18,1]{0,2,1:T(1,128)S(1)} %get-tuple-element.12), channel_id=1, source_target_pairs={{2,0},{4,2},{6,4},{3,1},{5,3},{7,5},{10,8},{12,10},{14,12},{11,9},... | collective-permute-start | bytes 13832 | tf_op jit(solution)/shard_map/ppermute | solution.py:18
  209.8 6.8 %collective-permute-start.12 = (f32[64,1,256]{0,2,1:T(8,128)S(1)}, f32[64,1,256]{0,2,1:T(8,128)S(1)}, u32[]{:S(2)}, u32[]{:S(2)}) collective-permute-start(f32[64,1,256]{0,2,1:T(8,128)S(1)} %get-tuple-element.15), channel_id=1, source_target_pairs={{0,1},{1,8},{8,9},{9,16},{16,17},{17,24},{24,25},{2,3},{3,10},{10,... | collective-permute-start | bytes 196616 | tf_op jit(solution)/shard_map/ppermute | solution.py:15
  214.1 7.1 %collective-permute-start.13 = (f32[64,1,256]{0,2,1:T(8,128)S(1)}, f32[64,1,256]{0,2,1:T(8,128)S(1)}, u32[]{:S(2)}, u32[]{:S(2)}) collective-permute-start(f32[64,1,256]{0,2,1:T(8,128)S(1)} %get-tuple-element.16), channel_id=1, source_target_pairs={{1,0},{8,1},{9,8},{16,9},{17,16},{24,17},{25,24},{3,2},{10,3},{11,... | collective-permute-start | bytes 196616 | tf_op jit(solution)/shard_map/ppermute | solution.py:18
  221.3 4.2 %collective-permute-start.14 = (f32[64,18,1]{0,2,1:T(1,128)S(1)}, f32[64,18,1]{0,2,1:T(1,128)S(1)}, u32[]{:S(2)}, u32[]{:S(2)}) collective-permute-start(f32[64,18,1]{0,2,1:T(1,128)S(1)} %get-tuple-element.9), channel_id=1, source_target_pairs={{0,2},{2,4},{4,6},{1,3},{3,5},{5,7},{8,10},{10,12},{12,14},{9,11},... | collective-permute-start | bytes 13832 | tf_op jit(solution)/shard_map/ppermute | solution.py:15
  224.2 3.8 %collective-permute-start.15 = (f32[64,18,1]{0,2,1:T(1,128)S(1)}, f32[64,18,1]{0,2,1:T(1,128)S(1)}, u32[]{:S(2)}, u32[]{:S(2)}) collective-permute-start(f32[64,18,1]{0,2,1:T(1,128)S(1)} %get-tuple-element.10), channel_id=1, source_target_pairs={{2,0},{4,2},{6,4},{3,1},{5,3},{7,5},{10,8},{12,10},{14,12},{11,9},... | collective-permute-start | bytes 13832 | tf_op jit(solution)/shard_map/ppermute | solution.py:18
Sparse Core Ops, SparseCore 0:
  26.6 91.6 all-reduce.2
  130.8 31.6 reduce-scatter.1
  234.7 33.6 all-gather.2
